TPU v7x, 32 devices: a whole 2x2x4 slice. The times are simulated.
32 devices in a mesh: seq: 16 (over z, x, core), grp: 2 (over y).
Axes of the slice: x: 2, y: 2, z: 4, core: 2. Of those that a mesh axis runs over, the one named last changes fastest.
Arguments:
- prefill_queries: bfloat16 [1024, 4096], P('seq', 'grp'), may hold values from -6 to 6
- prefill_keys: bfloat16 [1024, 512], P('seq', 'grp'), may hold values from -6 to 6
- prefill_values: bfloat16 [1024, 512], P('seq', 'grp'), may hold values from -6 to 6
- block_mask: int32 [16, 16], replicated, may hold values 0 or 1
- bit_widths: int32 [4], P('grp'), may hold values from 3 to 8
- scale_exps: int32 [4], P('grp'), may hold values from 1 to 4
- decode_queries: bfloat16 [4, 32, 4096], P(None, 'seq', 'grp'), may hold values from -6 to 6
- new_keys: bfloat16 [4, 32, 512], P(None, 'seq', 'grp'), may hold values from -6 to 6
- new_values: bfloat16 [4, 32, 512], P(None, 'seq', 'grp'), may hold values from -6 to 6
- context_len: int32 [32], P('seq'), may hold values from 1 to 1024
Outputs:
- prefill_out: bfloat16 [1024, 4096], P('seq', 'grp')
- decode_out: bfloat16 [4, 32, 4096], P(None, 'seq', 'grp')
All inputs are finite; a program needn't handle non-finite values.
Results may differ from a plain program's by a relative error of at most 0.012.
Values may be sent and summed in bfloat16 or wider, within the bound.
No kernel may reach another device: no remote copies, remote signals or barrier semaphores. Data moves between devices by JAX's collectives and lax.ppermute only.
A program may use at most 64 MiB of HBM per device.

v0:
```python
import math
import jax
import jax.numpy as jnp
from jax import lax
from jax.sharding import PartitionSpec as P

HEADS = 32
KV_HEADS = 4
HEAD = 128
STEPS = 4
very_low = -1e30
norm_eps = 1e-06


def sign_table(order):
    positions = jnp.arange(order, dtype=jnp.int32)
    common_bits = positions[:, None] & positions[None, :]
    parity = jnp.zeros((order, order), jnp.int32)
    for bit_number in range(order.bit_length() - 1):
        parity = parity + (common_bits >> bit_number & 1)
    return (1 - 2 * (parity % 2)).astype(jnp.float32)


def level_terms(bit_widths, scale_exps):
    clip_level = 2.0 ** (bit_widths.astype(jnp.float32) - 1.0) - 1.0
    forward = 2.0 ** scale_exps.astype(jnp.float32) / math.sqrt(HEAD)
    backward = 2.0 ** (-scale_exps.astype(jnp.float32)) / math.sqrt(HEAD)
    return (clip_level, forward, backward)


def online_update(carried, scores, allowed, values, pattern):
    running_max, weight_sum, weighted = carried
    masked = jnp.where(allowed, scores, very_low)
    new_max = jnp.maximum(running_max, jnp.max(masked, axis=-1))
    factor = jnp.exp(running_max - new_max)
    weights = jnp.where(allowed, jnp.exp(masked - new_max[..., None]), 0.0)
    weight_sum = weight_sum * factor + jnp.sum(weights, axis=-1)
    weighted = weighted * factor[..., None] + jnp.einsum(
        pattern, weights.astype(jnp.bfloat16), values, preferred_element_type=jnp.float32
    )
    return (new_max, weight_sum, weighted)


def in_blocks(fold_fn, carried, arrays, offset):
    count_rows = arrays[0].shape[0]
    block_rows = math.gcd(count_rows, 1024)
    if block_rows == count_rows or block_rows < 128:
        return fold_fn(carried, arrays, offset)
    number = count_rows // block_rows
    stacked = tuple((array.reshape((number, block_rows) + array.shape[1:]) for array in arrays))

    def advance(running, scan_item):
        position, pieces = scan_item
        return (fold_fn(running, pieces, offset + position * block_rows), None)

    carried, _ = lax.scan(advance, carried, (jnp.arange(number, dtype=jnp.int32), stacked))
    return carried


def local(
    prefill_queries,
    prefill_keys,
    prefill_values,
    block_mask,
    bit_widths,
    scale_exps,
    decode_queries,
    new_keys,
    new_values,
    context_len,
):
    local_tokens = prefill_queries.shape[0]
    kv_local = bit_widths.shape[0]
    group_size = HEADS // KV_HEADS
    row_count = context_len.shape[0]
    full_width = HEADS * HEAD
    score_scale = 1.0 / math.sqrt(HEAD)
    seq_index = lax.axis_index("seq")
    sign_matrix = sign_table(HEAD).astype(jnp.bfloat16)
    clip_level, forward, backward = level_terms(bit_widths, scale_exps)
    queries = prefill_queries.reshape(local_tokens, kv_local, group_size, HEAD)
    query_pos = seq_index * local_tokens + jnp.arange(local_tokens, dtype=jnp.int32)
    mask_row = block_mask[seq_index]
    block_ids = jnp.arange(mask_row.shape[0], dtype=jnp.int32)

    def encode(rows):
        shaped = rows.reshape(rows.shape[0], kv_local, HEAD)
        rotated = jnp.dot(shaped, sign_matrix, preferred_element_type=jnp.float32)
        levels = jnp.floor(rotated * forward[:, None] + 0.5)
        limited = jnp.clip(levels, -clip_level[:, None], clip_level[:, None])
        return limited.astype(jnp.bfloat16).reshape(rows.shape[0], kv_local * HEAD)

    def restore(rows):
        shaped = rows.reshape(rows.shape[0], kv_local, HEAD)
        restored = jnp.dot(shaped, sign_matrix, preferred_element_type=jnp.float32)
        return (restored * backward[:, None]).astype(jnp.bfloat16)

    def attend(carried, pieces, offset):
        key_rows, value_rows = pieces
        count_rows = key_rows.shape[0]
        key_shaped = key_rows.reshape(count_rows, kv_local, HEAD)
        value_shaped = value_rows.reshape(count_rows, kv_local, HEAD)
        scores = (
            jnp.einsum("tkgd,skd->tkgs", queries, key_shaped, preferred_element_type=jnp.float32)
            * score_scale
        )
        key_pos = offset + jnp.arange(count_rows, dtype=jnp.int32)
        key_block = key_pos // local_tokens
        block_open = jnp.sum(
            jnp.where(key_block[:, None] == block_ids[None, :], mask_row[None, :], 0), axis=1
        )
        allowed = (key_pos[None, :] <= query_pos[:, None]) & (
            (key_block == seq_index) | (block_open == 1)
        )[None, :]
        return online_update(
            carried, scores, allowed[:, None, None, :], value_shaped, "tkgs,skd->tkgd"
        )

    def attend_keep(carried, pieces, offset):
        running, key_store, value_store = carried
        running = in_blocks(attend, running, pieces, offset)
        key_store = encode(pieces[0])
        value_store = encode(pieces[1])
        return (running, key_store, value_store)

    start_shape = (local_tokens, kv_local, group_size)
    start_state = (
        jnp.full(start_shape, very_low, jnp.float32),
        jnp.zeros(start_shape, jnp.float32),
        jnp.zeros(start_shape + (HEAD,), jnp.float32),
    )
    empty_store = jnp.zeros((local_tokens * lax.axis_size("seq"), kv_local * HEAD), jnp.bfloat16)
    fold_fn, initial = (attend_keep, (start_state, empty_store, empty_store))
    folded = fold_fn(
        initial,
        (
            lax.all_gather(prefill_keys, "seq", axis=0, tiled=True),
            lax.all_gather(prefill_values, "seq", axis=0, tiled=True),
        ),
        jnp.int32(0),
    )
    dec_shaped = decode_queries.reshape(STEPS, row_count, kv_local, group_size, HEAD)

    def decode_step(carried, pieces, offset):
        key_rows, value_rows = pieces
        count_rows = key_rows.shape[0]
        key_plain = restore(key_rows)
        value_plain = restore(value_rows)
        scores = (
            jnp.einsum(
                "trkgd,pkd->trkgp", dec_shaped, key_plain, preferred_element_type=jnp.float32
            )
            * score_scale
        )
        key_pos = offset + jnp.arange(count_rows, dtype=jnp.int32)
        allowed = (key_pos[None, :] < context_len[:, None])[None, :, None, None, :]
        return online_update(carried, scores, allowed, value_plain, "trkgp,pkd->trkgd")

    dec_shape = (STEPS, row_count, kv_local, group_size)
    dec_state = (
        jnp.full(dec_shape, very_low, jnp.float32),
        jnp.zeros(dec_shape, jnp.float32),
        jnp.zeros(dec_shape + (HEAD,), jnp.float32),
    )
    prefill_state, key_store, value_store = folded
    dec_state = in_blocks(decode_step, dec_state, (key_store, value_store), jnp.int32(0))
    own_keys = new_keys.reshape(STEPS, row_count, kv_local, HEAD)
    own_values = new_values.reshape(STEPS, row_count, kv_local, HEAD)
    own_scores = (
        jnp.einsum("trkgd,urkd->trkgu", dec_shaped, own_keys, preferred_element_type=jnp.float32)
        * score_scale
    )
    step_pos = jnp.arange(STEPS, dtype=jnp.int32)
    own_open = (step_pos[None, :] <= step_pos[:, None])[:, None, None, None, :]
    dec_state = online_update(dec_state, own_scores, own_open, own_values, "trkgu,urkd->trkgd")
    prefill_attn = (prefill_state[2] / prefill_state[1][..., None]).reshape(
        local_tokens, kv_local * group_size * HEAD
    )
    decode_attn = (dec_state[2] / dec_state[1][..., None]).reshape(
        STEPS, row_count, kv_local * group_size * HEAD
    )
    prefill_squares, decode_squares = lax.psum(
        (
            jnp.sum(prefill_attn * prefill_attn, axis=-1),
            jnp.sum(decode_attn * decode_attn, axis=-1),
        ),
        "grp",
    )
    prefill_out = (
        prefill_attn * lax.rsqrt(prefill_squares[:, None] / full_width + norm_eps)
    ).astype(jnp.bfloat16)
    decode_out = (
        decode_attn * lax.rsqrt(decode_squares[..., None] / full_width + norm_eps)
    ).astype(jnp.bfloat16)
    return (prefill_out, decode_out)


def solution(mesh):
    placed = (
        P("seq", "grp"),
        P("seq", "grp"),
        P("seq", "grp"),
        P(),
        P("grp"),
        P("grp"),
        P(None, "seq", "grp"),
        P(None, "seq", "grp"),
        P(None, "seq", "grp"),
        P("seq"),
    )
    return jax.shard_map(
        local,
        mesh=mesh,
        in_specs=placed,
        out_specs=(P("seq", "grp"), P(None, "seq", "grp")),
        check_vma=False,
    )
```

profile of v0, /device:TPU:0, one launch (start us, length us, event | category | flops | bytes accessed | tf_op | source)
XLA Modules:
  0.0 64.8 jit_solution(13546898876530163890)
XLA Ops:
  0.6 0.0 copy-start
  0.6 0.0 copy-start.1
  0.7 0.7 %copy-done = s32[16,16]{1,0:T(8,128)S(1)} copy-done((s32[16,16]{1,0:T(8,128)S(1)}, s32[16,16]{1,0:T(8,128)}, u32[]{:S(2)}) %copy-start) | copy-done | bytes 1048
  1.3 0.7 %fusion.125 = (bf16[2]{0:T(256)(128)(2,1)S(1)}, bf16[2]{0:T(256)(128)(2,1)S(1)}) fusion(s32[2]{0:T(128)} %param.14), kind=kLoop, calls=%fused_computation.135 | loop fusion | flops 14 | bytes 16 | tf_op jit(solution)/shard_map/neg | solution.py:90
  2.0 0.7 %power_multiply_fusion.1 = (f32[2]{0:T(128)S(1)}, f32[2]{0:T(128)S(1)}) fusion(s32[2]{0:T(128)} %param.15), kind=kLoop, calls=%fused_computation.110 | loop fusion | flops 8 | bytes 24 | tf_op jit(solution)/shard_map/div | solution.py:26
  2.7 0.7 %iota_compare_fusion.2 = pred[2,1024]{1,0:T(4,128)(4,1)S(1)} fusion(s32[2]{0:T(128)} %param.19), kind=kLoop, calls=%fused_computation.94 | loop fusion | flops 2048 | bytes 2056 | tf_op jit(solution)/shard_map/lt | solution.py:156
  3.4 0.7 %reshape.186 = bf16[4,2,2,128]{3,2,1,0:T(2,128)(2,1)S(1)} reshape(bf16[4,2,256]{2,1,0:T(2,128)(2,1)} %param.17) | data formatting | bytes 8192 | tf_op jit(solution)/shard_map/reshape | solution.py:167
  4.1 0.7 %reshape.187 = bf16[4,2,2,128]{3,2,1,0:T(2,128)(2,1)S(1)} reshape(bf16[4,2,256]{2,1,0:T(2,128)(2,1)} %param.18) | data formatting | bytes 8192 | tf_op jit(solution)/shard_map/reshape | solution.py:168
  4.8 0.1 select_reduce_fusion
  4.9 0.8 %reshape.185 = bf16[4,2,2,8,128]{4,3,2,1,0:T(8,128)(2,1)S(1)} reshape(bf16[4,2,2048]{2,1,0:T(2,128)(2,1)} %param.16) | data formatting | bytes 65536 | tf_op jit(solution)/shard_map/reshape | solution.py:142
  5.7 0.3 fusion.128
  6.0 0.1 fusion.55
  6.1 1.0 %copy.148 = bf16[8,8,16,128]{3,2,1,0:T(8,128)(2,1)S(1)} copy(bf16[8,8,16,128]{3,1,2,0:T(8,128)(2,1)} %bitcast.106) | data formatting | bytes 524288
  7.1 24.8 %all_gather.6 = bf16[1024,256]{1,0:T(8,128)(2,1)S(1)} all-gather(bf16[64,256]{1,0:T(8,128)(2,1)} %param.11), channel_id=1, replica_groups=mesh['seq'=16,'grp'=2] {'seq'}, dimensions={0}, use_global_device_ids=true | all-gather | bytes 557056 | tf_op jit(solution)/shard_map/all_gather | solution.py:137
  31.9 0.2 copy.102
  32.1 0.7 %fusion.19 = bf16[1024,2,128,1,1]{2,0,4,3,1:T(8,128)(2,1)S(1)} fusion(bf16[1024,2,128]{0,2,1:T(8,128)(2,1)S(1)} %bitcast.100, bf16[2]{0:T(256)(128)(2,1)S(1)} %get-tuple-element.14, f32[2]{0:T(128)S(1)} %get-tuple-element.16, f32[2]{0:T(128)S(1)} %get-tuple-element.15, bf16[2]{0:T(256)(128)(2,1)S(1)} %get-tuple-element.13), kind=kOutput, calls=%fused_computation.24 | convolution fusion | flops 138018816 | bytes 1048600 | tf_op jit(solution)/shard_map/dot_general | solution.py:95
  32.9 0.4 fusion.129
  33.3 0.1 fusion.82
  33.4 0.2 fusion.48
  33.7 0.0 copy-done.1
  33.7 18.9 %all_gather.7 = bf16[1024,256]{1,0:T(8,128)(2,1)S(1)} all-gather(bf16[64,256]{1,0:T(8,128)(2,1)S(1)} %copy-done.1), channel_id=1, replica_groups=mesh['seq'=16,'grp'=2] {'seq'}, dimensions={0}, use_global_device_ids=true | all-gather | bytes 557056 | tf_op jit(solution)/shard_map/all_gather | solution.py:138
  52.6 0.2 copy.105
  52.8 0.7 %fusion.18 = bf16[1024,2,128,1,1]{2,0,4,3,1:T(8,128)(2,1)S(1)} fusion(bf16[1024,2,128]{0,2,1:T(8,128)(2,1)S(1)} %bitcast.104, bf16[2]{0:T(256)(128)(2,1)S(1)} %get-tuple-element.14, f32[2]{0:T(128)S(1)} %get-tuple-element.16, f32[2]{0:T(128)S(1)} %get-tuple-element.15, bf16[2]{0:T(256)(128)(2,1)S(1)} %get-tuple-element.13), kind=kOutput, calls=%fused_computation.23 | convolution fusion | flops 138018816 | bytes 1048600 | tf_op jit(solution)/shard_map/dot_general | solution.py:95
  53.5 0.3 fusion.33
  53.8 0.3 multiply_reduce_fusion.1
  54.2 0.9 %fusion = (f32[64,2,8]{0,2,1:T(8,128)S(1)}, f32[2,1024,64,8]{1,2,3,0:T(8,128)S(1)}) fusion(pred[64,1024]{1,0:T(8,128)(4,1)S(1)} %fusion.55, bf16[1024,2,128,1]{0,2,3,1:T(8,128)(2,1)S(1)} %bitcast.101, bf16[64,2,8,128]{3,2,1,0:T(8,128)(2,1)S(1)} %bitcast.103), kind=kOutput, calls=%fused_computation.2 | convolution fusion | flops 271580160 | bytes 5050368 | tf_op jit(solution)/shard_map/tkgd,skd->tkgs/dot_general | solution.py:104
  55.1 1.3 %fusion.1 = f32[64,2,8]{0,2,1:T(8,128)S(1)} fusion(f32[2,1024,64,8]{1,2,3,0:T(8,128)S(1)} %get-tuple-element.18, f32[64,2,8]{0,2,1:T(8,128)S(1)} %broadcast_maximum_fusion, pred[64,1024]{1,0:T(8,128)(4,1)S(1)} %fusion.55), kind=kLoop, calls=%fused_computation.3 | loop fusion | flops 5241856 | bytes 4268032 | tf_op jit(solution)/shard_map/reduce_sum | solution.py:37
  56.5 1.4 %multiply_reduce_fusion = (f32[64]{0:T(128)S(1)}, f32[64,2,8,128]{3,0,2,1:T(8,128)S(1)}) fusion(f32[64,2,8]{0,2,1:T(8,128)S(1)} %get-tuple-element.12, bf16[1024,2,128,1]{0,2,3,1:T(8,128)(2,1)S(1)} %bitcast.105, f32[2,1024,64,8]{1,2,3,0:T(8,128)S(1)} %get-tuple-element.18, f32[64,2,8]{0,2,1:T(8,128)S(1)} %broadcast_maximum_fusion, ...), kind=kOutput, calls=%fused_computation.53 | convolution fusion | flops 274202560 | bytes 5320960 | tf_op jit(solution)/shard_map/tkgs,skd->tkgd/dot_general | solution.py:38
  57.9 4.9 %all-reduce = (f32[64]{0:T(128)S(1)}, f32[4,2]{1,0:T(4,128)S(1)}) all-reduce(f32[64]{0:T(128)S(1)} %get-tuple-element.19, f32[4,2]{1,0:T(4,128)S(1)} %get-tuple-element.25), channel_id=1, replica_groups=mesh['seq'=16,'grp'=2] {'grp'}, use_global_device_ids=true, to_apply=%region_4.5 | all-reduce | flops 72 | bytes 576 | tf_op jit(solution)/shard_map/psum | solution.py:182
  62.8 0.7 %multiply_convert_fusion = bf16[4,2,2048]{2,1,0:T(2,128)(2,1)} fusion(f32[4,2,2048]{2,1,0:T(2,128)S(1)} %reshape.188, f32[4,2]{1,0:T(4,128)S(1)} %add_rsqrt_fusion), kind=kLoop, calls=%fused_computation.71 | loop fusion | flops 32768 | bytes 98336 | tf_op jit(solution)/shard_map/convert_element_type | solution.py:194
  63.6 0.3 copy.107
  63.9 0.9 %fusion.39 = bf16[64,2048]{1,0:T(8,128)(2,1)} fusion(f32[8,8,16,128]{3,2,1,0:T(8,128)S(1)} %bitcast.102, f32[64]{0:T(128)S(1)} %add_rsqrt_fusion.1), kind=kLoop, calls=%fused_computation.43 | loop fusion | flops 262144 | bytes 786688 | tf_op jit(solution)/shard_map/convert_element_type | solution.py:191
  (17 shorter events, 0.1 us)
Async XLA Ops:
  0.6 0.7 %copy-start = (s32[16,16]{1,0:T(8,128)S(1)}, s32[16,16]{1,0:T(8,128)}, u32[]{:S(2)}) copy-start(s32[16,16]{1,0:T(8,128)} %param.13) | copy-start | bytes 3076
  0.6 33.1 %copy-start.1 = (bf16[64,256]{1,0:T(8,128)(2,1)S(1)}, bf16[64,256]{1,0:T(8,128)(2,1)}, u32[]{:S(2)}) copy-start(bf16[64,256]{1,0:T(8,128)(2,1)} %param.12) | copy-start | bytes 98308
where the time goes:
time: 65.2 us; the launch traced here: 64.8 us
  blocking collectives  48.6 us (75%)
  other arithmetic  5.65 us (9%)
  matrix products  5.04 us (8%)
  local copies, waits for them, and re-layouts  4.63 us (7%)
  between operations  0.81 us (1%)
    all_gather x1, blocking collectives, local(): lax.all_gather(prefill_keys, 'seq', axis=0, tiled=True)  24.8 us
    all_gather x1, blocking collectives, local(): lax.all_gather(prefill_values, 'seq', axis=0, tiled=True)  18.9 us
    psum x1, blocking collectives, local(): lax.psum((jnp.sum(prefill_attn * prefill_attn, axis=-1), jnp.sum(decode_a...  4.93 us
    dot_general x3, matrix products, online_update(): jnp.einsum(pattern, weights.astype(jnp.bfloat16), values, preferred_eleme...  2.03 us
    unnamed x5, local copies, waits for them, and re-layouts  1.66 us
    reduce_sum x2, other arithmetic, online_update(): weight_sum = weight_sum * factor + jnp.sum(weights, axis=-1)  1.6 us
    dot_general x2, matrix products, restore(): restored = jnp.dot(shaped, sign_matrix, preferred_element_type=jnp.float32)  1.46 us

commit v1 on v0

--- a/solution.py
+++ b/solution.py
@@ -134,7 +134,10 @@
     folded = fold_fn(
         initial,
         (
-            lax.all_gather(prefill_keys, "seq", axis=0, tiled=True),
+            jnp.concatenate(
+                lax.all_to_all(jnp.stack([prefill_keys] * lax.axis_size("seq")), "seq", 0, 0),
+                axis=0,
+            ),
             lax.all_gather(prefill_values, "seq", axis=0, tiled=True),
         ),
         jnp.int32(0),

time: 65.2 us -> 52.8 us (0.81)
  blocking collectives: 48.6 us -> 28.4 us
  starting transfers between devices: 0 us -> 7.39 us
  local copies, waits for them, and re-layouts: 4.63 us -> 5.51 us
  other arithmetic: 5.65 us -> 4.98 us
    all_gather x1 -> x0, blocking collectives: 24.8 us -> none  [local(): lax.all_gather(prefill_keys, 'seq', axis=0, tiled=True)]
    all_to_all x0 -> x1, starting transfers between devices: none -> 7.39 us  [local(): lax.all_to_all(jnp.stack([prefill_keys] * lax.axis_size('seq')), 'seq', 0...]
    all_gather x1, blocking collectives: 18.9 us -> 23.5 us  [local(): lax.all_gather(prefill_values, 'seq', axis=0, tiled=True)]
    another operation x0 -> x2, local copies, waits for them, and re-layouts: none -> 1.73 us  [the longest x1 1.61 us: local(): jnp.stack([prefill_keys] * lax.axis_size('seq'))]
    unnamed x5, local copies, waits for them, and re-layouts: 1.66 us -> 1 us
    lt x1, other arithmetic: 0.73 us -> 0.08 us  [decode_step(): allowed = (key_pos[None, :] < context_len[:, None])[None, :, None, None, :]]
  transfers between devices with their start and end apart: 0 -> 1, of which waited for: 0 -> 0; matrix products, arithmetic and copies ran while one was open for 0% -> 11% of each run, Pallas kernels for 0% -> 0%
where the time goes in v1:
time: 52.8 us; the launch traced here: 52.3 us
  blocking collectives  28.4 us (54%)
  starting transfers between devices  7.39 us (14%)
  local copies, waits for them, and re-layouts  5.51 us (10%)
  matrix products  5.09 us (10%)
  other arithmetic  4.98 us (9%)
  between operations  0.85 us (2%)
    all_gather x1, blocking collectives, local(): lax.all_gather(prefill_values, 'seq', axis=0, tiled=True)  23.5 us
    all_to_all x1, starting transfers between devices, local(): lax.all_to_all(jnp.stack([prefill_keys] * lax.axis_size('seq')), 'seq', 0...  7.39 us
    psum x1, blocking collectives, local(): lax.psum((jnp.sum(prefill_attn * prefill_attn, axis=-1), jnp.sum(decode_a...  4.93 us
    dot_general x3, matrix products, online_update(): jnp.einsum(pattern, weights.astype(jnp.bfloat16), values, preferred_eleme...  2.03 us
    another operation x1, local copies, waits for them, and re-layouts, local(): jnp.stack([prefill_keys] * lax.axis_size('seq'))  1.61 us
    reduce_sum x2, other arithmetic, online_update(): weight_sum = weight_sum * factor + jnp.sum(weights, axis=-1)  1.59 us
    dot_general x2, matrix products, restore(): restored = jnp.dot(shaped, sign_matrix, preferred_element_type=jnp.float32)  1.45 us
  transfers between devices with their start and end apart: 1, of which 0 were waited for; matrix products, arithmetic and copies ran while one was open for 11% of the time, Pallas kernels for 0%

profile of v1, /device:TPU:0, one launch (start us, length us, event | category | flops | bytes accessed | tf_op | source)
XLA Modules:
  0.0 52.3 jit_solution(15541897155891013883)
XLA Ops:
  0.6 0.0 copy-start
  0.6 0.0 copy-start.1
  0.7 1.6 %stack.2 = bf16[16,64,256]{2,1,0:T(8,128)(2,1)} broadcast(bf16[64,256]{1,0:T(8,128)(2,1)} %param.11), dimensions={1,2} | broadcast | bytes 557056 | tf_op jit(solution)/shard_map/stack | solution.py:138
  2.3 7.4 %all-to-all-start = ((bf16[16,64,256]{2,1,0:T(8,128)(2,1)}), bf16[16,64,256]{2,1,0:T(8,128)(2,1)S(1)}, u32[]{:S(2)}, u32[]{:S(2)}) async-start(bf16[16,64,256]{2,1,0:T(8,128)(2,1)} %stack.2), calls=%async_computation | async-start | bytes 1048576 | tf_op jit(solution)/shard_map/all_to_all | solution.py:138
  9.7 0.7 %fusion.128 = (bf16[2]{0:T(256)(128)(2,1)S(1)}, bf16[2]{0:T(256)(128)(2,1)S(1)}) fusion(s32[2]{0:T(128)} %param.14), kind=kLoop, calls=%fused_computation.137 | loop fusion | flops 14 | bytes 16 | tf_op jit(solution)/shard_map/neg | solution.py:90
  10.4 0.7 %power_multiply_fusion.1 = (f32[2]{0:T(128)S(1)}, f32[2]{0:T(128)S(1)}) fusion(s32[2]{0:T(128)} %param.15), kind=kLoop, calls=%fused_computation.112 | loop fusion | flops 8 | bytes 24 | tf_op jit(solution)/shard_map/div | solution.py:26
  11.0 0.7 %reshape.183 = bf16[4,2,2,128]{3,2,1,0:T(2,128)(2,1)S(1)} reshape(bf16[4,2,256]{2,1,0:T(2,128)(2,1)} %param.17) | data formatting | bytes 8192 | tf_op jit(solution)/shard_map/reshape | solution.py:170
  11.7 0.7 %reshape.184 = bf16[4,2,2,128]{3,2,1,0:T(2,128)(2,1)S(1)} reshape(bf16[4,2,256]{2,1,0:T(2,128)(2,1)} %param.18) | data formatting | bytes 8192 | tf_op jit(solution)/shard_map/reshape | solution.py:171
  12.4 0.8 %reshape.182 = bf16[4,2,2,8,128]{4,3,2,1,0:T(8,128)(2,1)S(1)} reshape(bf16[4,2,2048]{2,1,0:T(2,128)(2,1)} %param.16) | data formatting | bytes 65536 | tf_op jit(solution)/shard_map/reshape | solution.py:145
  13.2 1.0 %copy.142 = bf16[8,8,16,128]{3,2,1,0:T(8,128)(2,1)S(1)} copy(bf16[8,8,16,128]{3,1,2,0:T(8,128)(2,1)} %bitcast.99) | data formatting | bytes 524288
  14.2 23.5 %all_gather.3 = bf16[1024,256]{1,0:T(8,128)(2,1)S(1)} all-gather(bf16[64,256]{1,0:T(8,128)(2,1)} %param.12), channel_id=1, replica_groups=mesh['seq'=16,'grp'=2] {'seq'}, dimensions={0}, use_global_device_ids=true | all-gather | bytes 557056 | tf_op jit(solution)/shard_map/all_gather | solution.py:141
  37.7 0.2 copy.100
  37.9 0.0 copy-done
  38.0 0.1 select_reduce_fusion
  38.0 0.7 %fusion.18 = bf16[1024,2,128,1,1]{2,0,4,3,1:T(8,128)(2,1)S(1)} fusion(bf16[1024,2,128]{0,2,1:T(8,128)(2,1)S(1)} %bitcast.97, bf16[2]{0:T(256)(128)(2,1)S(1)} %get-tuple-element.14, f32[2]{0:T(128)S(1)} %get-tuple-element.16, f32[2]{0:T(128)S(1)} %get-tuple-element.15, bf16[2]{0:T(256)(128)(2,1)S(1)} %get-tuple-element.13), kind=kOutput, calls=%fused_computation.23 | convolution fusion | flops 138018816 | bytes 1048600 | tf_op jit(solution)/shard_map/dot_general | solution.py:95
  38.8 0.0 copy-done.1
  38.8 0.1 iota_compare_fusion.2
  38.9 0.1 fusion.58
  39.0 0.3 fusion.131
  39.3 0.0 all-to-all-done
  39.3 0.1 reshape_reshape.4
  39.4 0.7 %fusion.19 = bf16[1024,2,128,1,1]{2,0,4,3,1:T(8,128)(2,1)S(1)} fusion(bf16[1024,2,128]{2,1,0:T(2,128)(2,1)S(1)} %reshape_reshape.4, bf16[2]{0:T(256)(128)(2,1)S(1)} %get-tuple-element.14, f32[2]{0:T(128)S(1)} %get-tuple-element.16, f32[2]{0:T(128)S(1)} %get-tuple-element.15, bf16[2]{0:T(256)(128)(2,1)S(1)} %get-tuple-element.13), kind=kOutput, calls=%fused_computation.24 | convolution fusion | flops 138018816 | bytes 1048600 | tf_op jit(solution)/shard_map/dot_general | solution.py:95
  40.2 0.4 fusion.132
  40.6 0.1 fusion.85
  40.7 0.2 fusion.52
  41.0 0.3 fusion.33
  41.3 0.3 multiply_reduce_fusion.1
  41.6 0.9 %fusion = (f32[64,2,8]{0,2,1:T(8,128)S(1)}, f32[2,1024,64,8]{1,2,3,0:T(8,128)S(1)}) fusion(pred[64,1024]{1,0:T(8,128)(4,1)S(1)} %fusion.58, bf16[64,2,8,128]{3,2,1,0:T(8,128)(2,1)S(1)} %bitcast.96, bf16[1024,2,128,1]{2,1,0,3:T(2,128)(2,1)S(1)} %bitcast.94), kind=kOutput, calls=%fused_computation.2 | convolution fusion | flops 271580160 | bytes 5050368 | tf_op jit(solution)/shard_map/tkgd,skd->tkgs/dot_general | solution.py:104
  42.6 1.3 %fusion.1 = f32[64,2,8]{0,2,1:T(8,128)S(1)} fusion(f32[2,1024,64,8]{1,2,3,0:T(8,128)S(1)} %get-tuple-element.18, f32[64,2,8]{0,2,1:T(8,128)S(1)} %broadcast_maximum_fusion, pred[64,1024]{1,0:T(8,128)(4,1)S(1)} %fusion.58), kind=kLoop, calls=%fused_computation.3 | loop fusion | flops 5241856 | bytes 4268032 | tf_op jit(solution)/shard_map/reduce_sum | solution.py:37
  44.0 1.4 %multiply_reduce_fusion = (f32[64]{0:T(128)S(1)}, f32[64,2,8,128]{3,0,2,1:T(8,128)S(1)}) fusion(f32[64,2,8]{0,2,1:T(8,128)S(1)} %get-tuple-element.12, bf16[1024,2,128,1]{0,2,3,1:T(8,128)(2,1)S(1)} %bitcast.98, f32[2,1024,64,8]{1,2,3,0:T(8,128)S(1)} %get-tuple-element.18, f32[64,2,8]{0,2,1:T(8,128)S(1)} %broadcast_maximum_fusion, ...), kind=kOutput, calls=%fused_computation.56 | convolution fusion | flops 274202560 | bytes 5320960 | tf_op jit(solution)/shard_map/tkgs,skd->tkgd/dot_general | solution.py:38
  45.4 4.9 %all-reduce = (f32[64]{0:T(128)S(1)}, f32[4,2]{1,0:T(4,128)S(1)}) all-reduce(f32[64]{0:T(128)S(1)} %get-tuple-element.19, f32[4,2]{1,0:T(4,128)S(1)} %get-tuple-element.25), channel_id=1, replica_groups=mesh['seq'=16,'grp'=2] {'grp'}, use_global_device_ids=true, to_apply=%region_4.5 | all-reduce | flops 72 | bytes 576 | tf_op jit(solution)/shard_map/psum | solution.py:185
  50.3 0.3 copy.102
  50.7 0.7 %multiply_convert_fusion = bf16[4,2,2048]{2,1,0:T(2,128)(2,1)} fusion(f32[4,2,2048]{2,1,0:T(2,128)S(1)} %reshape.185, f32[4,2]{1,0:T(4,128)S(1)} %add_rsqrt_fusion), kind=kLoop, calls=%fused_computation.73 | loop fusion | flops 32768 | bytes 98336 | tf_op jit(solution)/shard_map/convert_element_type | solution.py:197
  51.4 0.9 %fusion.39 = bf16[64,2048]{1,0:T(8,128)(2,1)} fusion(f32[8,8,16,128]{3,2,1,0:T(8,128)S(1)} %bitcast.95, f32[64]{0:T(128)S(1)} %add_rsqrt_fusion.1), kind=kLoop, calls=%fused_computation.43 | loop fusion | flops 262144 | bytes 786688 | tf_op jit(solution)/shard_map/convert_element_type | solution.py:194
  (17 shorter events, 0.2 us)
Async XLA Ops:
  0.6 37.3 %copy-start = (s32[16,16]{1,0:T(8,128)S(1)}, s32[16,16]{1,0:T(8,128)}, u32[]{:S(2)}) copy-start(s32[16,16]{1,0:T(8,128)} %param.13) | copy-start | bytes 3076
  0.6 38.1 %copy-start.1 = (s32[2]{0:T(128)S(1)}, s32[2]{0:T(128)}, u32[]{:S(2)}) copy-start(s32[2]{0:T(128)} %param.19) | copy-start | bytes 28
  2.3 37.0 %all-to-all-start = ((bf16[16,64,256]{2,1,0:T(8,128)(2,1)}), bf16[16,64,256]{2,1,0:T(8,128)(2,1)S(1)}, u32[]{:S(2)}, u32[]{:S(2)}) async-start(bf16[16,64,256]{2,1,0:T(8,128)(2,1)} %stack.2), calls=%async_computation | async-start | bytes 1048576 | tf_op jit(solution)/shard_map/all_to_all | solution.py:138
